TPU v7x, 256 devices: a whole 4x4x8 slice. The times are simulated.
256 devices in a mesh: rows: 8 (over z_lo, x), feat: 32 (over y, z_hi, core).
Axes of the slice: x: 4, y: 4, z: 8 (z_hi: 4, z_lo: 2; z = z_hi * 2 + z_lo), core: 2. Of those that a mesh axis runs over, the one named last changes fastest.
Arguments:
- slab_grads: bfloat16 [1792, 262144], P('rows', 'feat'), may hold values from -6 to 6
- basis: bfloat16 [262144, 1024], P('feat', 'rows'), may hold values from -0.01171875 to 0.01171875
- eigenvalues: float32 [1024], replicated, may hold values from 0.02 to 2
- store_rows: bfloat16 [131072, 1024], P(('rows', 'feat')), may hold values from -0.1875 to 0.1875
- slab_index: int32 [1792], replicated, may hold values from 0 to 131071
Outputs:
- scores: float32 [1792, 131072], P(None, ('rows', 'feat'))
All inputs are finite; a program needn't handle non-finite values.
Results may differ from a plain program's by a relative error of at most 0.0029.
Values may be sent and summed in bfloat16 or wider, within the bound.
A program may use at most 128 MiB of HBM per device.

v0:
```python
import jax
import jax.numpy as jnp
from jax import lax
from jax.sharding import Mesh
from jax.sharding import PartitionSpec as P

FEAT = ("feat_0", "feat_1", "feat_2")
ROWS_FEAT = ("rows", "feat_0", "feat_1", "feat_2")


DAMPING = 0.1


def cut_along(x, dim, peers):
    shape = x.shape
    parts = x.reshape(*shape[:dim], peers, shape[dim] // peers, *shape[dim + 1 :])
    return jnp.moveaxis(parts, dim, 0)


def sum_at_owner(x, axis, dim):
    parts = cut_along(x, dim, lax.axis_size(axis))
    arrived = lax.all_to_all(parts, axis, split_axis=0, concat_axis=0, tiled=True)
    return arrived.sum(axis=0)


def summed_rows(x, axes, dim):
    far, near = axes
    parts = cut_along(x, dim, lax.axis_size(far))
    nearer = sum_at_owner(parts, near, dim + 1)
    arrived = lax.all_to_all(nearer, far, split_axis=0, concat_axis=0, tiled=True)
    return arrived.sum(axis=0)


def filled_up(lines, peers):
    spare = -lines.shape[0] % peers
    if not spare:
        return lines
    return jnp.concatenate([lines, jnp.zeros((spare, *lines.shape[1:]), lines.dtype)])


def sent_to_all(x, axis):
    copies = jnp.broadcast_to(x, (lax.axis_size(axis), *x.shape))
    return lax.all_to_all(copies, axis, split_axis=0, concat_axis=0, tiled=True)


def in_order(parts, dim):
    parts = jnp.moveaxis(parts, 0, dim)
    shape = parts.shape
    return parts.reshape(*shape[:dim], shape[dim] * shape[dim + 1], *shape[dim + 2 :])


def gathered_by_axis(x, axes, dim):
    far, near = axes
    first = sent_to_all(x, far)
    parts = jnp.swapaxes(sent_to_all(first, near), 0, 1)
    return in_order(parts.reshape(-1, *x.shape), dim)


def total_of(x, axes):
    lines = x.reshape(-1, x.shape[-1])
    own = summed_rows(filled_up(lines, lax.axis_size(axes[0]) * lax.axis_size(axes[1])), axes, 0)
    whole = gathered_by_axis(own, axes, 0)
    return whole[: len(lines)].reshape(x.shape)


def shards(slab_grads, basis, eigenvalues, store_rows, slab_index):
    feat_groups = lax.axis_size(FEAT)
    store_count = store_rows.shape[0]
    first_column = (lax.axis_index("rows") * feat_groups + lax.axis_index(FEAT)) * store_count
    columns = first_column + jnp.arange(store_count, dtype=jnp.int32)
    partial_value = jnp.dot(
        slab_grads,
        lax.all_gather(basis, "rows", axis=1, tiled=True),
        preferred_element_type=jnp.float32,
    )
    summed = total_of(partial_value, (("feat_0", "feat_1"), "feat_2"))
    whitened = (summed / (eigenvalues + DAMPING)).astype(jnp.bfloat16)
    product = lax.dot_general(
        lax.all_gather(whitened, "rows", axis=0, tiled=True),
        store_rows,
        (((1,), (1,)), ((), ())),
        preferred_element_type=jnp.float32,
    )
    return jnp.where(slab_index[:, None] == columns[None, :], jnp.zeros_like(product), product)


def solution(mesh):
    split = Mesh(
        mesh.devices.reshape(mesh.shape["rows"], 4, 4, 2), ("rows", "feat_0", "feat_1", "feat_2")
    )
    placed = (P("rows", FEAT), P(FEAT, "rows"), P(), P(ROWS_FEAT, None), P())
    return jax.shard_map(
        shards, mesh=split, in_specs=placed, out_specs=P(None, ROWS_FEAT), check_vma=False
    )
```

profile of v0, /device:TPU:1, one launch (start us, length us, event | category | flops | bytes accessed | tf_op | source)
XLA Modules:
  0.0 322.2 jit_solution(14432967977835595114)
XLA Ops:
  6.5 0.0 copy-start
  6.5 0.0 all-gather.3.cloned.1.call-start
  6.5 0.7 all-gather.3.cloned.1.call-update
  7.3 181.8 %all-gather.3.cloned.1.call-done = bf16[8192,1024]{1,0:T(8,128)(2,1)} async-done(((bf16[8192,128]{1,0:T(8,128)(2,1)}), bf16[8192,1024]{1,0:T(8,128)(2,1)}) %all-gather.3.cloned.1.call-update) | async-done | bytes 16777232 | tf_op jit(solution)/shard_map/all_gather | solution.py:73
  189.1 8.9 %fusion = f32[224,1024]{1,0:T(8,128)S(1)} fusion(bf16[224,8192]{1,0:T(8,128)(2,1)} %param.5, bf16[8192,1024]{1,0:T(8,128)(2,1)} %all-gather.3.cloned.1.call-done), kind=kOutput, calls=%fused_computation.4 | convolution fusion | flops 3758096384 | bytes 21364736 | tf_op jit(solution)/shard_map/dot_general | solution.py:71
  198.0 0.1 reshape_reshape.6
  198.1 0.5 copy.11
  198.6 0.0 copy-start.1
  198.6 7.8 %all_to_all.20 = f32[2,16,7,1024]{3,1,2,0:T(8,128)S(1)} all-to-all(f32[2,16,7,1024]{3,1,2,0:T(8,128)S(1)} %copy.11), channel_id=1, replica_groups=mesh['rows'=8,'feat_0'=4,'feat_1'=4,'feat_2'=2] {'feat_2'}, dimensions={0} | all-to-all | bytes 1835008 | tf_op jit(solution)/shard_map/all_to_all | solution.py:22
  206.4 0.1 reduce_sum.18
  206.5 0.3 copy.12
  206.8 26.4 %all_to_all.21 = f32[16,7,1024]{2,1,0:T(8,128)S(1)} all-to-all(f32[16,7,1024]{2,1,0:T(8,128)S(1)} %copy.12), channel_id=1, replica_groups=mesh['rows'=8,'feat_0'=4,'feat_1'=4,'feat_2'=2] {'feat_0','feat_1'}, dimensions={0} | all-to-all | bytes 917504 | tf_op jit(solution)/shard_map/all_to_all | solution.py:30
  233.3 0.8 broadcast_in_dim.13
  234.1 4.5 %all-to-all-start.2 = ((f32[16,7,1024]{2,1,0:T(8,128)}), f32[16,7,1024]{2,1,0:T(8,128)S(1)}, u32[]{:S(2)}, u32[]{:S(2)}) async-start(f32[16,7,1024]{2,1,0:T(8,128)} %broadcast_in_dim.13), calls=%async_computation.2 | async-start | bytes 1048576 | tf_op jit(solution)/shard_map/all_to_all | solution.py:43
  238.6 0.0 all-gather.5.cloned.1.call-start
  238.6 0.0 copy-done.1
  238.7 16.7 %all-to-all-done.2 = f32[16,7,1024]{2,1,0:T(8,128)S(1)} async-done(((f32[16,7,1024]{2,1,0:T(8,128)}), f32[16,7,1024]{2,1,0:T(8,128)S(1)}, u32[]{:S(2)}, u32[]{:S(2)}) %all-to-all-start.2) | async-done | bytes 458784 | tf_op jit(solution)/shard_map/all_to_all | solution.py:43
  255.4 0.3 copy.13
  255.6 0.1 broadcast_in_dim.14
  255.7 0.0 copy-start.2
  255.7 6.4 %all_to_all.22 = f32[2,16,7,1024]{3,1,2,0:T(8,128)S(1)} all-to-all(f32[2,16,7,1024]{3,1,2,0:T(8,128)S(1)} %broadcast_in_dim.14), channel_id=1, replica_groups=mesh['rows'=8,'feat_0'=4,'feat_1'=4,'feat_2'=2] {'feat_2'}, dimensions={0} | all-to-all | bytes 1835008 | tf_op jit(solution)/shard_map/all_to_all | solution.py:43
  262.1 0.5 copy.14
  262.7 0.1 reshape_reshape.7
  262.8 0.9 divide_convert_fusion
  263.7 0.0 all-gather.5.cloned.1.call-update
  263.7 45.6 %all-gather.5.cloned.1.call-done = bf16[1792,1024]{1,0:T(8,128)(2,1)} async-done(((bf16[224,1024]{1,0:T(8,128)(2,1)}), bf16[1792,1024]{1,0:T(8,128)(2,1)}) %all-gather.5.cloned.1.call-update) | async-done | bytes 3670032 | tf_op jit(solution)/shard_map/all_gather | solution.py:79
  309.4 0.0 copy-done
  309.4 0.0 copy-done.2
  309.4 6.0 %compare_select_fusion = f32[1792,512]{1,0:T(8,128)} fusion(bf16[1792,1024]{1,0:T(8,128)(2,1)} %all-gather.5.cloned.1.call-done, bf16[512,1024]{1,0:T(8,128)(2,1)S(1)} %copy-done, s32[512]{0:T(512)S(1)} %iota_add_fusion, s32[1792]{0:T(1024)S(1)} %copy-done.2), kind=kOutput, calls=%fused_computation | convolution fusion | flops 1880883200 | bytes 8397824 | tf_op jit(solution)/shard_map/dot_general | solution.py:78
  (3 shorter events, 0.1 us)
Async XLA Ops:
  6.5 302.8 %copy-start = (bf16[512,1024]{1,0:T(8,128)(2,1)S(1)}, bf16[512,1024]{1,0:T(8,128)(2,1)}, u32[]{:S(2)}) copy-start(bf16[512,1024]{1,0:T(8,128)(2,1)} %param.8) | copy-start | bytes 3145732
  6.5 182.5 %all-gather.3.cloned.1.call-start = ((), (), s32[]{:S(2)}) async-start(), calls=%async_computation.4 | async-start | bytes 18874368 | tf_op jit(solution)/shard_map/all_gather | solution.py:73
  198.6 40.0 %copy-start.1 = (f32[1024]{0:T(1024)S(1)}, f32[1024]{0:T(1024)}, u32[]{:S(2)}) copy-start(f32[1024]{0:T(1024)} %param.7) | copy-start | bytes 12292
  234.1 21.2 %all-to-all-start.2 = ((f32[16,7,1024]{2,1,0:T(8,128)}), f32[16,7,1024]{2,1,0:T(8,128)S(1)}, u32[]{:S(2)}, u32[]{:S(2)}) async-start(f32[16,7,1024]{2,1,0:T(8,128)} %broadcast_in_dim.13), calls=%async_computation.2 | async-start | bytes 1048576 | tf_op jit(solution)/shard_map/all_to_all | solution.py:43
  238.6 70.8 %all-gather.5.cloned.1.call-start = ((), (), s32[]{:S(2)}) async-start(), calls=%async_computation.5 | async-start | bytes 4128768 | tf_op jit(solution)/shard_map/all_gather | solution.py:79
  255.7 53.6 %copy-start.2 = (s32[1792]{0:T(1024)S(1)}, s32[1792]{0:T(1024)}, u32[]{:S(2)}) copy-start(s32[1792]{0:T(1024)} %param.9) | copy-start | bytes 21508
Sparse Core Ops, SparseCore 0:
  9.1 179.9 all-gather.2
  263.8 45.5 all-gather.4
where the time goes:
time: 323 us; the launch traced here: 322 us
  waiting for transfers between devices  245 us (76%)
  blocking collectives  40.6 us (13%)
  matrix products  14.9 us (5%)
  between operations  13.5 us (4%)
  starting transfers between devices  4.5 us (1%)
    all_gather x1, waiting for transfers between devices, shards(): lax.all_gather(basis, 'rows', axis=1, tiled=True)  182 us
    all_gather x1, waiting for transfers between devices, shards(): lax.all_gather(whitened, 'rows', axis=0, tiled=True)  45.6 us
    all_to_all x1, blocking collectives, summed_rows(): lax.all_to_all(nearer, far, split_axis=0, concat_axis=0, tiled=True)  26.4 us
    all_to_all x1, waiting for transfers between devices, sent_to_all(): return lax.all_to_all(copies, axis, split_axis=0, concat_axis=0, tiled=True)  16.7 us
    dot_general x1, matrix products, shards(): jnp.dot(slab_grads, lax.all_gather(basis, 'rows', axis=1, tiled=True), pr...  8.88 us
    all_to_all x1, blocking collectives, sum_at_owner(): lax.all_to_all(parts, axis, split_axis=0, concat_axis=0, tiled=True)  7.78 us
  transfers between devices with their start and end apart: 3, of which 3 were waited for; matrix products, arithmetic and copies ran while one was open for 0% of the time, Pallas kernels for 0%

commit v1 on v0

v1 whole, which is shorter than its diff:
```python
import jax
import jax.numpy as jnp
from jax import lax
from jax.experimental import pallas as pl
from jax.experimental.pallas import tpu as pltpu
from jax.sharding import Mesh
from jax.sharding import PartitionSpec as P

AXES = ("zl", "x", "y", "zh", "core")
SIZES = {"zl": 2, "x": 4, "y": 4, "zh": 4, "core": 2}
MESH = pl.DeviceIdType.MESH
DAMPING = 0.1
CHUNKS = 8
PIECE = 56
LANES = 128


def turned(axis, by):
    return lax.rem(lax.axis_index(axis) + (by % SIZES[axis]), SIZES[axis])


def project_kernel(
    g, b, eig, w,
    g_own, g_pair, b_all, acc, core_in, part, y_in, y_sum, z_in,
    local_sem, g_send, g_recv, b_send, b_recv, f_send, f_recv,
    c_send, c_recv, y_send, y_recv, z_send, z_recv, w_send, w_recv,
):
    rows, feats = g.shape
    step = feats // CHUNKS
    zl, x, y, zh, core = (lax.axis_index(a) for a in AXES)
    pair = {"zl": 1 - zl}
    sibling = {"core": 1 - core}
    right, left, across = {"x": turned("x", 1)}, {"x": turned("x", -1)}, {"x": turned("x", 2)}
    y_peers = [{"y": turned("y", d)} for d in (1, 3, 2)]
    zh_peers = [{"zh": turned("zh", d)} for d in (1, 3, 2)]
    z_peers = (
        [pair]
        + zh_peers
        + [{"zl": 1 - zl, "zh": turned("zh", d)} for d in (1, 3, 2)]
    )

    barrier = pltpu.get_barrier_semaphore()
    everyone = [pair, right, left, across, sibling] + y_peers + z_peers[1:]
    for peer in everyone:
        pl.semaphore_signal(barrier, inc=1, device_id=peer, device_id_type=MESH)
    own_g = pltpu.make_async_copy(g, g_own, local_sem.at[0])
    own_b = pltpu.make_async_copy(b, b_all.at[0], local_sem.at[1])
    own_g.start()
    own_b.start()
    pl.semaphore_wait(barrier, len(everyone))

    def remote(src, dst, send, recv, peer):
        return pltpu.make_async_remote_copy(
            src_ref=src, dst_ref=dst, send_sem=send, recv_sem=recv,
            device_id=peer, device_id_type=MESH,
        )

    def part_of(k):
        return pl.ds(pl.multiple_of(k * step, step), step)

    def g_copy(k):
        return remote(g.at[:, part_of(k)], g_pair.at[:, part_of(k)], g_send.at[k], g_recv.at[k], pair)

    def b_copy(side, k):
        peer = right if side == 0 else left
        return remote(
            b.at[part_of(k)], b_all.at[1 + side, part_of(k)],
            b_send.at[side, k], b_recv.at[side, k], peer,
        )

    def forward(side, k):
        peer = right if side == 0 else left
        return remote(
            b_all.at[1 + side, part_of(k)], b_all.at[3, part_of(k)],
            f_send.at[k], f_recv.at[k], peer,
        )

    @pl.loop(0, CHUNKS)
    def _(k):
        b_copy(0, k).start()
        b_copy(1, k).start()
        g_copy(k).start()

    acc[...] = jnp.zeros_like(acc)
    own_g.wait()
    own_b.wait()

    @pl.loop(0, CHUNKS // 2)
    def _(pairs):
        for odd in (0, 1):
            k = pairs * 2 + odd
            b_copy(0, k).wait_recv()
            b_copy(1, k).wait_recv()
            forward(odd, k).start()
            many = jnp.concatenate([b_all[i, part_of(k)] for i in (0, 1, 2)], axis=1)
            acc[0, :, : 3 * LANES] += jnp.dot(
                g_own[:, part_of(k)], many, preferred_element_type=jnp.float32
            )

    @pl.loop(0, CHUNKS)
    def _(k):
        forward(0, k).wait_recv()
        acc[0, :, 3 * LANES :] += jnp.dot(
            g_own[:, part_of(k)], b_all[3, part_of(k)], preferred_element_type=jnp.float32
        )

    @pl.loop(0, CHUNKS)
    def _(k):
        g_copy(k).wait_recv()
        many = jnp.concatenate([b_all[i, part_of(k)] for i in range(4)], axis=1)
        acc[1] += jnp.dot(g_pair[:, part_of(k)], many, preferred_element_type=jnp.float32)

    swap = remote(acc.at[1 - core], core_in, c_send.at[0], c_recv.at[0], sibling)
    swap.start()
    swap.wait_recv()
    for q in range(4):
        for p in range(4):
            piece = (slice(q * PIECE, (q + 1) * PIECE), slice(p * LANES, (p + 1) * LANES))
            part[q, p] = acc[(core, *piece)] + core_in[piece]

    y_copies = [
        remote(part.at[turned("y", d)], y_in.at[i], y_send.at[i], y_recv.at[i], y_peers[i])
        for i, d in enumerate((1, 3, 2))
    ]
    for copy in y_copies:
        copy.start()
    for copy in y_copies:
        copy.wait_recv()
    y_sum[...] = part[y] + y_in[0] + y_in[1] + y_in[2]

    z_copies = [
        remote(y_sum.at[turned("zh", d)], z_in.at[i], z_send.at[i], z_recv.at[i], zh_peers[i])
        for i, d in enumerate((1, 3, 2))
    ]
    for copy in z_copies:
        copy.start()
    for copy in z_copies:
        copy.wait_recv()
    total = y_sum[zh] + z_in[0] + z_in[1] + z_in[2]

    turn = jnp.where(zh == 0, 0, jnp.where(zh == 1, 3, jnp.where(zh == 2, 1, 2)))
    column = zl * 4 + lax.rem(x + turn, 4)
    row_half = lax.rem(zl + core, 2)
    scale = eig[pl.ds(column, 1), :] + DAMPING
    own = w.at[column, row_half * 4 + x, y]
    own[...] = (total / scale).astype(w.dtype)

    counter = [0]

    def spread(src, peer):
        i = counter[0]
        counter[0] += 1
        copy = remote(src, src, w_send.at[i], w_recv.at[i], peer)
        copy.start()
        return copy

    gathers = []

    def settle(copies):
        for copy in copies:
            copy.wait_recv()
        gathers.extend(copies)

    low, high = slice(0, 4), slice(4, 8)
    settle([spread(own, peer) for peer in z_peers])
    low_half, high_half = core, 1 - core
    settle(
        [spread(w.at[low, low_half * 4 + x, y], peer) for peer in y_peers]
        + [spread(w.at[high, high_half * 4 + x, y], peer) for peer in (right, left, across)]
    )

    def low_block(turn):
        return low_half * 4 + turned("x", turn)

    high_rows = pl.ds(high_half * 4, 4)
    near = [
        spread(w.at[low, low_block(0)], right),
        spread(w.at[low, low_block(0)], left),
        spread(w.at[high, high_rows, y], y_peers[0]),
        spread(w.at[high, high_rows, y], y_peers[1]),
    ]
    settle(near)
    settle(
        [
            spread(w.at[slice(0, 2), low_block(-1)], right),
            spread(w.at[slice(2, 4), low_block(1)], left),
            spread(w.at[slice(4, 6), high_rows, turned("y", -1)], y_peers[0]),
            spread(w.at[slice(6, 8), high_rows, turned("y", 1)], y_peers[1]),
        ]
    )
    settle(
        [
            spread(w.at[low, pl.ds(low_half * 4, 4)], sibling),
            spread(w.at[high, high_rows], sibling),
        ]
    )

    @pl.loop(0, CHUNKS // 2)
    def _(pairs):
        for odd in (0, 1):
            k = pairs * 2 + odd
            g_copy(k).wait_send()
            b_copy(0, k).wait_send()
            b_copy(1, k).wait_send()
            forward(odd, k).wait_send()

    swap.wait_send()
    for copy in y_copies + z_copies + gathers:
        copy.wait_send()


def project(g, b, eig):
    rows, feats = g.shape
    blocks = 8
    anywhere = pl.BlockSpec(memory_space=pl.ANY)
    vmem = pl.BlockSpec(memory_space=pltpu.VMEM)
    dma = pltpu.SemaphoreType.DMA
    f32, bf16 = jnp.float32, jnp.bfloat16
    return pl.pallas_call(
        project_kernel,
        out_shape=jax.ShapeDtypeStruct((blocks, blocks, 4, PIECE, LANES), bf16),
        in_specs=[anywhere, anywhere, vmem],
        out_specs=vmem,
        scratch_shapes=[
            pltpu.VMEM((rows, feats), bf16),
            pltpu.VMEM((rows, feats), bf16),
            pltpu.VMEM((4, feats, LANES), bf16),
            pltpu.VMEM((2, rows, 4 * LANES), f32),
            pltpu.VMEM((rows, 4 * LANES), f32),
            pltpu.VMEM((4, 4, PIECE, LANES), f32),
            pltpu.VMEM((3, 4, PIECE, LANES), f32),
            pltpu.VMEM((4, PIECE, LANES), f32),
            pltpu.VMEM((3, PIECE, LANES), f32),
            dma((2,)),
            dma((CHUNKS,)), dma((CHUNKS,)),
            dma((2, CHUNKS)), dma((2, CHUNKS)),
            dma((CHUNKS,)), dma((CHUNKS,)),
            dma((1,)), dma((1,)),
            dma((3,)), dma((3,)),
            dma((3,)), dma((3,)),
            dma((24,)), dma((24,)),
        ],
        compiler_params=pltpu.CompilerParams(
            collective_id=0, has_side_effects=True, vmem_limit_bytes=50 << 20
        ),
    )(g, b, eig)


ROW_TILE = 256


def score_kernel(first, w, store, index, out):
    columns = out.shape[1]
    wide = jnp.concatenate([w[i] for i in range(w.shape[0])], axis=1)
    product = lax.dot_general(
        wide, store[...], (((1,), (1,)), ((), ())), preferred_element_type=jnp.float32
    )
    here = first[0] + lax.broadcasted_iota(jnp.int32, (LANES, columns), 1)
    for i in range(ROW_TILE // LANES):
        line = index[pl.program_id(0), pl.ds(i, 1), :]
        wanted = jnp.broadcast_to(line, (LANES, LANES)).T
        wanted = jnp.concatenate([wanted] * (columns // LANES), axis=1)
        rows = slice(i * LANES, (i + 1) * LANES)
        out[rows, :] = jnp.where(wanted == here, 0.0, product[rows])


def score(first, w, store, index):
    blocks, count, lanes = w.shape
    columns, depth = store.shape
    tiles = count // ROW_TILE
    return pl.pallas_call(
        score_kernel,
        out_shape=jax.ShapeDtypeStruct((count, columns), jnp.float32),
        grid=(tiles,),
        in_specs=[
            pl.BlockSpec(memory_space=pltpu.SMEM),
            pl.BlockSpec((blocks, ROW_TILE, lanes), lambda i: (0, i, 0)),
            pl.BlockSpec((columns, depth), lambda i: (0, 0)),
            pl.BlockSpec((tiles, ROW_TILE // LANES, LANES), lambda i: (0, 0, 0)),
        ],
        out_specs=pl.BlockSpec((ROW_TILE, columns), lambda i: (i, 0)),
        compiler_params=pltpu.CompilerParams(vmem_limit_bytes=40 << 20),
    )(first, w, store, index)


def shards(slab_grads, basis, eigenvalues, store_rows, slab_index):
    zl, x, y, zh, core = (lax.axis_index(a) for a in AXES)
    place = (((zl * 4 + x) * 4 + y) * 4 + zh) * 2 + core
    first = (place * store_rows.shape[0]).astype(jnp.int32).reshape(1)
    w = project(slab_grads, basis, eigenvalues.reshape(8, LANES))
    w = w.reshape(8, 8 * 4 * PIECE, LANES)
    index = slab_index.reshape(-1, ROW_TILE // LANES, LANES)
    return score(first, w, store_rows, index)


def solution(mesh):
    split = Mesh(mesh.devices.reshape(2, 4, 4, 4, 2), AXES)
    rows, feat = ("zl", "x"), ("y", "zh", "core")
    placed = (P(rows, feat), P(feat, rows), P(), P(rows + feat, None), P())
    return jax.shard_map(
        shards, mesh=split, in_specs=placed, out_specs=P(None, rows + feat), check_vma=False
    )
```

time: 323 us -> 144 us (0.45)
  waiting for transfers between devices: 245 us -> 0 us
  Pallas kernels: 0 us -> 139 us
  blocking collectives: 40.6 us -> 0 us
  matrix products: 14.9 us -> 0 us
  between operations: 13.5 us -> 0.03 us
  starting transfers between devices: 4.5 us -> 0 us
    all_gather x2 -> x0, waiting for transfers between devices: 227 us -> none  [the longest x1 182 us: shards(): lax.all_gather(basis, 'rows', axis=1, tiled=True)]
    pallas_call x0 -> x2, Pallas kernels: none -> 139 us  [the longest x1 134 us: project(): pl.pallas_call(project_kernel, out_shape=jax.ShapeDtypeStruct((blocks, bl...]
    all_to_all x3 -> x0, blocking collectives: 40.6 us -> none  [the longest x1 26.4 us: summed_rows(): lax.all_to_all(nearer, far, split_axis=0, concat_axis=0, tiled=True)]
    all_to_all x1 -> x0, waiting for transfers between devices: 16.7 us -> none  [sent_to_all(): return lax.all_to_all(copies, axis, split_axis=0, concat_axis=0, tiled=True)]
    dot_general x2 -> x0, matrix products: 14.9 us -> none  [the longest x1 8.88 us: shards(): jnp.dot(slab_grads, lax.all_gather(basis, 'rows', axis=1, tiled=True), pr...]
    all_to_all x1 -> x0, starting transfers between devices: 4.46 us -> none  [sent_to_all(): return lax.all_to_all(copies, axis, split_axis=0, concat_axis=0, tiled=True)]
    unnamed x6 -> x8, local copies, waits for them, and re-layouts: 0.02 us -> 4.31 us
  transfers between devices with their start and end apart: 3 -> 0, of which waited for: 3 -> 0; matrix products, arithmetic and copies ran while one was open for 0% -> 0% of each run, Pallas kernels for 0% -> 0%
where the time goes in v1:
time: 144 us
  Pallas kernels  139 us (97%)
  local copies, waits for them, and re-layouts  5.02 us (3%)
    pallas_call x1, Pallas kernels, project(): pl.pallas_call(project_kernel, out_shape=jax.ShapeDtypeStruct((blocks, bl...  134 us
    pallas_call x1, Pallas kernels, score(): pl.pallas_call(score_kernel, out_shape=jax.ShapeDtypeStruct((count, colum...  5.22 us
    unnamed x8, local copies, waits for them, and re-layouts  4.31 us

profile of v1, /device:TPU:1, one launch (start us, length us, event | category | flops | bytes accessed | tf_op | source)
XLA Modules:
  0.0 144.2 jit_solution(6138388426976306685)
XLA Ops:
  0.0 0.7 reshape.15.index
  0.7 0.0 copy-start.1
  0.7 1.6 %copy-done.1 = bf16[8192,128]{1,0:T(8,128)(2,1)S(1)} copy-done((bf16[8192,128]{1,0:T(8,128)(2,1)S(1)}, bf16[8192,128]{1,0:T(8,128)(2,1)}, u32[]{:S(2)}) %copy-start.1) | copy-done | bytes 2097176
  2.3 0.0 copy-start.3
  2.3 0.7 copy-done.3
  3.0 0.0 copy-start.2
  3.0 133.9 %shard_map.55 = bf16[8,8,4,56,128]{4,3,2,1,0:T(8,128)(2,1)} custom-call(bf16[224,8192]{1,0:T(8,128)(2,1)} %g.1, bf16[8192,128]{1,0:T(8,128)(2,1)S(1)} %copy-done.1, f32[8,128]{1,0:T(8,128)S(1)} %bitcast.4), custom_call_target="tpu_custom_call" | custom-call | tf_op jit(solution)/shard_map/pallas_call | solution.py:219
  136.9 0.0 copy-done.2
  136.9 0.0 copy-start
  136.9 2.0 %copy-done = bf16[8,8,4,56,128]{4,3,2,1,0:T(8,128)(2,1)S(1)} copy-done((bf16[8,8,4,56,128]{4,3,2,1,0:T(8,128)(2,1)S(1)}, bf16[8,8,4,56,128]{4,3,2,1,0:T(8,128)(2,1)}, u32[]{:S(2)}) %copy-start) | copy-done | bytes 3670040
  138.9 5.2 %shard_map.56 = f32[1792,512]{1,0:T(8,128)} custom-call(s32[1]{0:T(128)} %bitcast.first, bf16[8,1792,128]{2,1,0:T(8,128)(2,1)S(1)} %bitcast.3, bf16[512,1024]{1,0:T(8,128)(2,1)S(1)} %copy-done.2, s32[7,2,128]{2,1,0:T(2,128)S(1)} %reshape.15.index), custom_call_target="tpu_custom_call" | custom-call | tf_op jit(solution)/shard_map/pallas_call | solution.py:271
Async XLA Ops:
  0.7 1.6 %copy-start.1 = (bf16[8192,128]{1,0:T(8,128)(2,1)S(1)}, bf16[8192,128]{1,0:T(8,128)(2,1)}, u32[]{:S(2)}) copy-start(bf16[8192,128]{1,0:T(8,128)(2,1)} %b.1) | copy-start | bytes 6291460
  2.3 0.7 copy-start.3
  3.0 133.9 %copy-start.2 = (bf16[512,1024]{1,0:T(8,128)(2,1)S(1)}, bf16[512,1024]{1,0:T(8,128)(2,1)}, u32[]{:S(2)}) copy-start(bf16[512,1024]{1,0:T(8,128)(2,1)} %store.1) | copy-start | bytes 3145732
  136.9 2.0 %copy-start = (bf16[8,8,4,56,128]{4,3,2,1,0:T(8,128)(2,1)S(1)}, bf16[8,8,4,56,128]{4,3,2,1,0:T(8,128)(2,1)}, u32[]{:S(2)}) copy-start(bf16[8,8,4,56,128]{4,3,2,1,0:T(8,128)(2,1)} %shard_map.55) | copy-start | bytes 11010052

commit v2 on v0

v2 whole, which is shorter than its diff:
```python
import jax
import jax.numpy as jnp
from jax import lax
from jax.experimental import pallas as pl
from jax.experimental.pallas import tpu as pltpu
from jax.sharding import Mesh
from jax.sharding import PartitionSpec as P

AXES = ("zl", "x", "y", "zh", "core")
SIZES = {"zl": 2, "x": 4, "y": 4, "zh": 4, "core": 2}
MESH = pl.DeviceIdType.MESH
DAMPING = 0.1
CHUNKS = 8
LANES = 128
TILE = 8
BLOCK = 64
TURNS = (0, -1, 1, 2)
NEAR_ROWS = ((0, 32), (32, 96), (96, 160))
LAST_ROWS = (160, 224)
EARLY, ACROSS, FIFTH, SIXTH = (0, 5, 0, 3), (0, 5, 3, 4), (5, 6, 0, 4), (6, 7, 0, 4)
BATCHES = (EARLY, ACROSS, FIFTH, SIXTH)


def turned(axis, by):
    return lax.rem(lax.axis_index(axis) + (by % SIZES[axis]), SIZES[axis])


def project_kernel(
    g, b, eig_in, w,
    eig, g_own, g_pair, b_all, acc, r1, s1, r2,
    local_sem, g_send, g_recv, b_send, b_recv, f_send, f_recv,
    a_send, a_recv, c_send, c_recv, e_send, e_recv, h_send, h_recv, k_send, k_recv,
):
    rows, feats = g.shape
    step = feats // CHUNKS
    zl, x, y, zh, core = (lax.axis_index(a) for a in AXES)
    pair, sibling = {"zl": 1 - zl}, {"core": 1 - core}
    right, left = {"x": turned("x", 1)}, {"x": turned("x", -1)}
    mine = core * 4 + y

    plane = [(dy, dc) for dy in (2, 1, 3) for dc in (0, 1)] + [(0, 1)]
    deep = [2, 1, 3]
    column = [(dl, dh) for dh in (2, 1, 3, 0) for dl in (0, 1) if dl or dh]
    sheet = [(dx, dy) for dx in (2, 1, 3, 0) for dy in (2, 1, 3, 0) if dx or dy]

    def flipped(value, by):
        return 1 - value if by else value

    def plane_peer(o):
        return {"y": turned("y", o[0]), "core": flipped(core, o[1])}

    def column_peer(o):
        return {"zl": flipped(zl, o[0]), "zh": turned("zh", o[1])}

    def sheet_peer(o):
        return {"x": turned("x", o[0]), "y": turned("y", o[1])}

    barrier = pltpu.get_barrier_semaphore()
    everyone = (
        [column_peer(o) for o in column]
        + [sheet_peer(o) for o in sheet]
        + [plane_peer(o) for o in plane if o[1]]
    )
    for peer in everyone:
        pl.semaphore_signal(barrier, inc=1, device_id=peer, device_id_type=MESH)
    locals_ = [
        pltpu.make_async_copy(b, b_all.at[0], local_sem.at[0]),
        pltpu.make_async_copy(g, g_own, local_sem.at[1]),
        pltpu.make_async_copy(eig_in, eig, local_sem.at[2]),
    ]
    for copy in locals_:
        copy.start()
    pl.semaphore_wait(barrier, len(everyone))

    def remote(src, dst, send, recv, peer):
        return pltpu.make_async_remote_copy(
            src_ref=src, dst_ref=dst, send_sem=send, recv_sem=recv,
            device_id=peer, device_id_type=MESH,
        )

    def part_of(k):
        return pl.ds(pl.multiple_of(k * step, step), step)

    def near_copy(i):
        lines = slice(*NEAR_ROWS[i])
        return remote(g.at[lines], g_pair.at[lines], g_send.at[i], g_recv.at[i], pair)

    def last_copy(k):
        place = (slice(*LAST_ROWS), part_of(k))
        return remote(g.at[place], g_pair.at[place], g_send.at[3 + k], g_recv.at[3 + k], pair)

    def b_copy(side, k):
        return remote(
            b.at[part_of(k)], b_all.at[1 + side, part_of(k)],
            b_send.at[side, k], b_recv.at[side, k], left if side else right,
        )

    def forward(side, k):
        return remote(
            b_all.at[1 + side, part_of(k)], b_all.at[3, part_of(k)],
            f_send.at[k], f_recv.at[k], left if side else right,
        )

    near_copy(0).start()
    for i in range(1, 3):
        near_copy(i).start()

    @pl.loop(0, CHUNKS)
    def _(k):
        b_copy(0, k).start()
        b_copy(1, k).start()
        last_copy(k).start()

    def dot(lhs, rhs):
        out = jnp.dot(lhs, rhs, preferred_element_type=jnp.float32)
        return out.reshape(-1, TILE, out.shape[1])

    def joined(places, k):
        return jnp.concatenate([b_all[i, part_of(k)] for i in places], axis=1)

    def add_own(k, rhs, lanes):
        out = dot(g_own[:, part_of(k)], rhs)
        acc[0:3, :, :, lanes] += out[:24].reshape(3, 8, TILE, -1)
        acc[3, 0:4, :, lanes] += out[24:]

    def add_pair(k, rhs, lanes):
        out = dot(g_pair[0:96, part_of(k)], rhs)
        acc[3, 4:8, :, lanes] += out[:4]
        acc[4, :, :, lanes] += out[4:]

    def add_block(block, k):
        first = block * BLOCK - rows
        out = dot(g_pair[first : first + BLOCK, part_of(k)], joined(range(4), k))
        acc[block] += out

    acc[...] = jnp.zeros_like(acc)
    for copy in locals_:
        copy.wait()

    started = []

    def go(copy):
        copy.start()
        started.append(copy)
        return copy

    def lanes_of(batch):
        return slice(batch[2] * LANES, batch[3] * LANES)

    def reduce_plane(n):
        batch = BATCHES[n]
        blocks, lanes = slice(*batch[:2]), lanes_of(batch)
        copies = []
        for i, o in enumerate(plane):
            peer = plane_peer(o)
            theirs = peer["core"] * 4 + peer["y"]
            copies.append(
                go(remote(
                    acc.at[blocks, theirs, :, lanes], r1.at[i, blocks, :, lanes],
                    a_send.at[n, i], a_recv.at[n, i], peer,
                ))
            )
        return copies

    def within(place, batch):
        if batch[2:] == (0, 4):
            return None
        return jnp.logical_and(place >= batch[2], place < batch[3])

    def guarded(condition, body):
        if condition is None:
            body()
        else:
            pl.when(condition)(body)

    def deep_copy(n, i):
        batch = BATCHES[n]
        blocks, there = slice(*batch[:2]), turned("zh", deep[i])
        return remote(
            s1.at[there, blocks], r2.at[i, blocks], c_send.at[n, i], c_recv.at[n, i], {"zh": there}
        )

    def reduce_deep(n, copies):
        batch = BATCHES[n]
        blocks = slice(*batch[:2])
        for copy in copies:
            copy.wait_recv()
        for p in range(batch[2], batch[3]):
            lanes = slice(p * LANES, (p + 1) * LANES)
            total = acc[blocks, mine, :, lanes]
            for i in range(len(plane)):
                total = total + r1[i, blocks, :, lanes]
            s1[p, blocks] = total
        for i in range(len(deep)):
            guarded(within(turned("zh", deep[i]), batch), lambda i=i: deep_copy(n, i).start())

    def own_place(n):
        return w.at[zl, zh, x, slice(*BATCHES[n][:2]), mine]

    def column_copy(n, i):
        place = own_place(n)
        return remote(place, place, e_send.at[n, i], e_recv.at[n, i], column_peer(column[i]))

    def spread_column(n):
        batch = BATCHES[n]
        blocks = slice(*batch[:2])

        def body():
            for i in range(len(deep)):
                deep_copy(n, i).wait_recv()
            total = s1[zh, blocks]
            for i in range(len(deep)):
                total = total + r2[i, blocks]
            turn = jnp.where(zh == 0, 0, jnp.where(zh == 1, 3, jnp.where(zh == 2, 1, 2)))
            scale = eig[pl.ds(zl * 4 + lax.rem(x + turn, 4), 1), :] + DAMPING
            own_place(n)[...] = (total / scale[None]).astype(w.dtype)
            for i in range(len(column)):
                column_copy(n, i).start()

        guarded(within(zh, batch), body)

    def spread_sheet(n):
        batch = BATCHES[n]
        for i, (_, dh) in enumerate(column):
            guarded(
                within(turned("zh", -dh), batch), lambda i=i: column_copy(n, i).wait_recv()
            )
        place = w.at[:, slice(*batch[2:]), x, slice(*batch[:2]), mine]
        return [
            go(remote(place, place, h_send.at[n, i], h_recv.at[n, i], sheet_peer(o)))
            for i, o in enumerate(sheet)
        ]

    def share(n, copies):
        batch = BATCHES[n]
        for copy in copies:
            copy.wait_recv()
        place = w.at[:, slice(*batch[2:]), :, slice(*batch[:2]), pl.ds(core * 4, 4)]
        return go(remote(place, place, k_send.at[n], k_recv.at[n], sibling))

    @pl.loop(0, CHUNKS // 2)
    def _(pairs):
        for odd in (0, 1):
            k = pairs * 2 + odd
            b_copy(0, k).wait_recv()
            b_copy(1, k).wait_recv()
            forward(odd, k).start()
            add_own(k, joined(range(3), k), slice(0, 3 * LANES))

    near_copy(0).wait_recv()
    near_copy(1).wait_recv()

    @pl.loop(0, CHUNKS)
    def _(k):
        add_pair(k, joined(range(3), k), slice(0, 3 * LANES))

    early = reduce_plane(0)
    reduce_deep(0, early)
    spread_column(0)

    @pl.loop(0, CHUNKS)
    def _(k):
        forward(0, k).wait_recv()
        add_own(k, b_all[3, part_of(k)], slice(3 * LANES, 4 * LANES))
        add_pair(k, b_all[3, part_of(k)], slice(3 * LANES, 4 * LANES))

    across = reduce_plane(1)
    near_copy(2).wait_recv()

    @pl.loop(0, CHUNKS)
    def _(k):
        add_block(5, k)

    fifth = reduce_plane(2)
    early = spread_sheet(0)
    reduce_deep(1, across)
    reduce_deep(2, fifth)

    @pl.loop(0, CHUNKS)
    def _(k):
        last_copy(k).wait_recv()
        add_block(6, k)

    sixth = reduce_plane(3)
    spread_column(1)
    spread_column(2)
    reduce_deep(3, sixth)
    across = spread_sheet(1)
    fifth = spread_sheet(2)
    spread_column(3)
    shares = [share(0, early)]
    sixth = spread_sheet(3)
    shares += [share(1, across), share(2, fifth), share(3, sixth)]
    for copy in shares:
        copy.wait_recv()

    for i in range(3):
        near_copy(i).wait_send()

    @pl.loop(0, CHUNKS)
    def _(k):
        last_copy(k).wait_send()
        b_copy(0, k).wait_send()
        b_copy(1, k).wait_send()
        forward(0, k).wait_send()

    for n, batch in enumerate(BATCHES):
        for i in range(len(deep)):
            guarded(within(turned("zh", deep[i]), batch), lambda: deep_copy(n, i).wait_send())

        def body():
            for i in range(len(column)):
                column_copy(n, i).wait_send()

        guarded(within(zh, batch), body)
    for copy in started:
        copy.wait_send()


def project(g, b, eig):
    rows, feats = g.shape
    hbm = pl.BlockSpec(memory_space=pltpu.HBM)
    vmem = pl.BlockSpec(memory_space=pltpu.VMEM)
    dma = pltpu.SemaphoreType.DMA
    f32, bf16 = jnp.float32, jnp.bfloat16
    count = len(BATCHES)
    return pl.pallas_call(
        project_kernel,
        out_shape=pltpu.VMEM((2, 4, 4, 7, 8, TILE, LANES), bf16),
        in_specs=[hbm, hbm, hbm],
        out_specs=vmem,
        scratch_shapes=[
            pltpu.VMEM(eig.shape, f32),
            pltpu.VMEM((rows, feats), bf16),
            pltpu.VMEM((rows, feats), bf16),
            pltpu.VMEM((4, feats, LANES), bf16),
            pltpu.VMEM((7, 8, TILE, 4 * LANES), f32),
            pltpu.VMEM((7, 7, TILE, 4 * LANES), f32),
            pltpu.VMEM((4, 7, TILE, LANES), f32),
            pltpu.VMEM((3, 7, TILE, LANES), f32),
            dma((3,)),
            dma((3 + CHUNKS,)), dma((3 + CHUNKS,)),
            dma((2, CHUNKS)), dma((2, CHUNKS)),
            dma((CHUNKS,)), dma((CHUNKS,)),
            dma((count, 7)), dma((count, 7)),
            dma((count, 3)), dma((count, 3)),
            dma((count, 7)), dma((count, 7)),
            dma((count, 15)), dma((count, 15)),
            dma((count,)), dma((count,)),
        ],
        compiler_params=pltpu.CompilerParams(
            collective_id=0, has_side_effects=True, vmem_limit_bytes=40 << 20
        ),
    )(*(pltpu.with_memory_space_constraint(a, pltpu.HBM) for a in (g, b, eig)))


HALF = 224


def score_kernel(first, w, store, index, out):
    columns = out.shape[1]
    half = pl.program_id(0) // 4
    x = lax.rem(pl.program_id(0), 4)
    here = first[0] + lax.broadcasted_iota(jnp.int32, (LANES, columns), 1)

    def tile(shift):
        wide = []
        for q in range(2):
            lines = pl.ds(pl.multiple_of((half if q == 0 else 1 - half) * HALF, 32), HALF)
            for c in range(4):
                p = [t % 4 for t in TURNS].index((c - shift) % 4)
                wide.append(w[q, p, shift, lines])
        return jnp.concatenate(wide, axis=1)

    for shift in range(4):

        @pl.when(x == shift)
        def _():
            product = lax.dot_general(
                tile(shift), store[...], (((1,), (1,)), ((), ())),
                preferred_element_type=jnp.float32,
            )
            out[...] = product

    for start in range(0, HALF, LANES):
        count = min(LANES, HALF - start)
        line = index[pl.program_id(0), :, start : start + LANES]
        wanted = jnp.broadcast_to(line, (LANES, LANES)).T[:count]
        wanted = jnp.concatenate([wanted] * (columns // LANES), axis=1)
        lines = slice(start, start + count)
        out[lines, :] = jnp.where(wanted == here[:count], 0.0, out[lines, :])


def score(first, w, store, index):
    columns, depth = store.shape
    count = index.shape[0] * HALF
    return pl.pallas_call(
        score_kernel,
        out_shape=jax.ShapeDtypeStruct((count, columns), jnp.float32),
        grid=(index.shape[0],),
        in_specs=[
            pl.BlockSpec(memory_space=pltpu.SMEM),
            pl.BlockSpec(memory_space=pltpu.VMEM),
            pl.BlockSpec(memory_space=pltpu.VMEM),
            pl.BlockSpec(memory_space=pltpu.VMEM),
        ],
        out_specs=pl.BlockSpec((HALF, columns), lambda i: (i, 0)),
        compiler_params=pltpu.CompilerParams(vmem_limit_bytes=24 << 20),
    )(first, w, store, index)


def shards(slab_grads, basis, eigenvalues, store_rows, slab_index):
    zl, x, y, zh, core = (lax.axis_index(a) for a in AXES)
    place = (((zl * 4 + x) * 4 + y) * 4 + zh) * 2 + core
    first = (place * store_rows.shape[0]).astype(jnp.int32).reshape(1)
    w = project(slab_grads, basis, eigenvalues.reshape(8, LANES))
    w = w.reshape(2, 4, 4, 7 * BLOCK, LANES)
    index = jnp.pad(slab_index.reshape(8, 1, HALF), ((0, 0), (0, 0), (0, 2 * LANES - HALF)))
    return score(first, w, store_rows, index)


def solution(mesh):
    split = Mesh(mesh.devices.reshape(2, 4, 4, 4, 2), AXES)
    rows, feat = ("zl", "x"), ("y", "zh", "core")
    placed = (P(rows, feat), P(feat, rows), P(), P(rows + feat, None), P())
    return jax.shard_map(
        shards, mesh=split, in_specs=placed, out_specs=P(None, rows + feat), check_vma=False
    )
```

time: 323 us -> 143 us (0.44)
  waiting for transfers between devices: 245 us -> 0 us
  Pallas kernels: 0 us -> 142 us
  blocking collectives: 40.6 us -> 0 us
  matrix products: 14.9 us -> 0 us
  between operations: 13.5 us -> 0.03 us
  starting transfers between devices: 4.5 us -> 0 us
    all_gather x2 -> x0, waiting for transfers between devices: 227 us -> none  [the longest x1 182 us: shards(): lax.all_gather(basis, 'rows', axis=1, tiled=True)]
    pallas_call x0 -> x2, Pallas kernels: none -> 142 us  [the longest x1 136 us: project(): pl.pallas_call(project_kernel, out_shape=pltpu.VMEM((2, 4, 4, 7, 8, TILE,...]
    all_to_all x3 -> x0, blocking collectives: 40.6 us -> none  [the longest x1 26.4 us: summed_rows(): lax.all_to_all(nearer, far, split_axis=0, concat_axis=0, tiled=True)]
    all_to_all x1 -> x0, waiting for transfers between devices: 16.7 us -> none  [sent_to_all(): return lax.all_to_all(copies, axis, split_axis=0, concat_axis=0, tiled=True)]
    dot_general x2 -> x0, matrix products: 14.9 us -> none  [the longest x1 8.88 us: shards(): jnp.dot(slab_grads, lax.all_gather(basis, 'rows', axis=1, tiled=True), pr...]
    all_to_all x1 -> x0, starting transfers between devices: 4.46 us -> none  [sent_to_all(): return lax.all_to_all(copies, axis, split_axis=0, concat_axis=0, tiled=True)]
  transfers between devices with their start and end apart: 3 -> 0, of which waited for: 3 -> 0; matrix products, arithmetic and copies ran while one was open for 0% -> 0% of each run, Pallas kernels for 0% -> 0%
where the time goes in v2:
time: 143 us
  Pallas kernels  142 us (99%)
    pallas_call x1, Pallas kernels, project(): pl.pallas_call(project_kernel, out_shape=pltpu.VMEM((2, 4, 4, 7, 8, TILE,...  136 us
    pallas_call x1, Pallas kernels, score(): pl.pallas_call(score_kernel, out_shape=jax.ShapeDtypeStruct((count, colum...  6.1 us

profile of v2, /device:TPU:1, one launch (start us, length us, event | category | flops | bytes accessed | tf_op | source)
XLA Modules:
  0.0 142.9 jit_solution(4369035777895358692)
XLA Ops:
  0.0 0.8 reshape.15
  0.8 0.0 copy-start
  0.8 136.0 %shard_map.55 = bf16[2,4,4,7,8,8,128]{6,5,4,3,2,1,0:T(8,128)(2,1)S(1)} custom-call(bf16[224,8192]{1,0:T(8,128)(2,1)} %g.1, bf16[8192,128]{1,0:T(8,128)(2,1)} %b.1, f32[8,128]{1,0:T(8,128)} %bitcast.4), custom_call_target="tpu_custom_call" | custom-call | tf_op jit(solution)/shard_map/pallas_call | solution.py:327
  136.8 0.0 copy-done
  136.8 6.1 %shard_map.56 = f32[1792,512]{1,0:T(8,128)} custom-call(s32[1]{0:T(128)} %bitcast.first, bf16[2,4,4,448,128]{4,3,2,1,0:T(8,128)(2,1)S(1)} %bitcast.3, bf16[512,1024]{1,0:T(8,128)(2,1)S(1)} %copy-done, s32[8,1,256]{2,1,0:T(1,128)S(1)} %pad.4.index), custom_call_target="tpu_custom_call" | custom-call | tf_op jit(solution)/shard_map/pallas_call | solution.py:397
  (1 shorter events, 0.0 us)
Async XLA Ops:
  0.8 136.0 %copy-start = (bf16[512,1024]{1,0:T(8,128)(2,1)S(1)}, bf16[512,1024]{1,0:T(8,128)(2,1)}, u32[]{:S(2)}) copy-start(bf16[512,1024]{1,0:T(8,128)(2,1)} %store.1) | copy-start | bytes 3145732

commit v3 on v2

--- a/solution.py
+++ b/solution.py
@@ -27,7 +27,7 @@
 
 def project_kernel(
     g, b, eig_in, w,
-    eig, g_own, g_pair, b_all, acc, r1, s1, r2,
+    eig, g_own, g_pair, b_all, acc, r1, s1, r2, w0, w1, w2, w3,
     local_sem, g_send, g_recv, b_send, b_recv, f_send, f_recv,
     a_send, a_recv, c_send, c_recv, e_send, e_recv, h_send, h_recv, k_send, k_recv,
 ):
@@ -138,6 +138,7 @@
         copy.wait()
 
     started = []
+    parts = (w0, w1, w2, w3)
 
     def go(copy):
         copy.start()
@@ -195,10 +196,14 @@
             guarded(within(turned("zh", deep[i]), batch), lambda i=i: deep_copy(n, i).start())
 
     def own_place(n):
-        return w.at[zl, zh, x, slice(*BATCHES[n][:2]), mine]
+        return parts[n].at[x, mine, zl, zh - BATCHES[n][2]]
 
     def column_copy(n, i):
         place = own_place(n)
+        return remote(place, place, e_send.at[n, i], e_recv.at[n, i], column_peer(column[i]))
+
+    def column_arrival(n, i):
+        place = parts[n].at[x, mine, 0, 0]
         return remote(place, place, e_send.at[n, i], e_recv.at[n, i], column_peer(column[i]))
 
     def spread_column(n):
@@ -213,7 +218,7 @@
                 total = total + r2[i, blocks]
             turn = jnp.where(zh == 0, 0, jnp.where(zh == 1, 3, jnp.where(zh == 2, 1, 2)))
             scale = eig[pl.ds(zl * 4 + lax.rem(x + turn, 4), 1), :] + DAMPING
-            own_place(n)[...] = (total / scale[None]).astype(w.dtype)
+            parts[n][x, mine, zl, zh - batch[2]] = (total / scale[None]).astype(w.dtype)
             for i in range(len(column)):
                 column_copy(n, i).start()
 
@@ -223,20 +228,30 @@
         batch = BATCHES[n]
         for i, (_, dh) in enumerate(column):
             guarded(
-                within(turned("zh", -dh), batch), lambda i=i: column_copy(n, i).wait_recv()
+                within(turned("zh", -dh), batch), lambda i=i: column_arrival(n, i).wait_recv()
             )
-        place = w.at[:, slice(*batch[2:]), x, slice(*batch[:2]), mine]
+        place = parts[n].at[x, mine]
         return [
             go(remote(place, place, h_send.at[n, i], h_recv.at[n, i], sheet_peer(o)))
             for i, o in enumerate(sheet)
         ]
 
     def share(n, copies):
-        batch = BATCHES[n]
         for copy in copies:
             copy.wait_recv()
-        place = w.at[:, slice(*batch[2:]), :, slice(*batch[:2]), pl.ds(core * 4, 4)]
+        place = parts[n].at[:, pl.ds(core * 4, 4)]
         return go(remote(place, place, k_send.at[n], k_recv.at[n], sibling))
+
+    def place_tiles(n, copy):
+        first, last, low, high = BATCHES[n]
+        copy.wait_recv()
+
+        @pl.loop(0, 32)
+        def _(i):
+            row, lot = i // 8, lax.rem(i, 8)
+            for q in range(2):
+                for p in range(low, high):
+                    w[q, p, row, first:last, lot] = parts[n][row, lot, q, p - low]
 
     @pl.loop(0, CHUNKS // 2)
     def _(pairs):
@@ -288,11 +303,14 @@
     across = spread_sheet(1)
     fifth = spread_sheet(2)
     spread_column(3)
-    shares = [share(0, early)]
+    early = share(0, early)
     sixth = spread_sheet(3)
-    shares += [share(1, across), share(2, fifth), share(3, sixth)]
-    for copy in shares:
-        copy.wait_recv()
+    place_tiles(0, early)
+    across = share(1, across)
+    fifth = share(2, fifth)
+    place_tiles(1, across)
+    place_tiles(2, fifth)
+    place_tiles(3, share(3, sixth))
 
     for i in range(3):
         near_copy(i).wait_send()
@@ -338,6 +356,10 @@
             pltpu.VMEM((7, 7, TILE, 4 * LANES), f32),
             pltpu.VMEM((4, 7, TILE, LANES), f32),
             pltpu.VMEM((3, 7, TILE, LANES), f32),
+            *(
+                pltpu.VMEM((4, 8, 2, high - low, last - first, TILE, LANES), bf16)
+                for first, last, low, high in BATCHES
+            ),
             dma((3,)),
             dma((3 + CHUNKS,)), dma((3 + CHUNKS,)),
             dma((2, CHUNKS)), dma((2, CHUNKS)),
@@ -355,56 +377,60 @@
 
 
 HALF = 224
+STEPS = 4
 
 
 def score_kernel(first, w, store, index, out):
     columns = out.shape[1]
-    half = pl.program_id(0) // 4
-    x = lax.rem(pl.program_id(0), 4)
-    here = first[0] + lax.broadcasted_iota(jnp.int32, (LANES, columns), 1)
-
-    def tile(shift):
-        wide = []
+    here = first[0] + lax.broadcasted_iota(jnp.int32, (HALF, LANES), 1)
+
+    def wide(half, x):
+        pieces = []
         for q in range(2):
-            lines = pl.ds(pl.multiple_of((half if q == 0 else 1 - half) * HALF, 32), HALF)
+            start = (half if q == 0 else 1 - half) * HALF
             for c in range(4):
-                p = [t % 4 for t in TURNS].index((c - shift) % 4)
-                wide.append(w[q, p, shift, lines])
-        return jnp.concatenate(wide, axis=1)
-
-    for shift in range(4):
-
-        @pl.when(x == shift)
+                p = [t % 4 for t in TURNS].index((c - x) % 4)
+                pieces.append(w[q, p, x, start : start + HALF])
+        return jnp.concatenate(pieces, axis=1)
+
+    def wanted(block):
+        lines, stop = [], (block + 1) * HALF
+        row = block * HALF
+        while row < stop:
+            tile = row // LANES * LANES
+            end = min(stop, tile + LANES)
+            line = index[tile : tile + LANES].reshape(1, LANES)
+            lines.append(jnp.broadcast_to(line, (LANES, LANES)).T[row - tile : end - tile])
+            row = end
+        return jnp.concatenate(lines, axis=0)
+
+    for step in range(STEPS):
+
+        @pl.when(pl.program_id(0) == step)
         def _():
-            product = lax.dot_general(
-                tile(shift), store[...], (((1,), (1,)), ((), ())),
-                preferred_element_type=jnp.float32,
-            )
-            out[...] = product
-
-    for start in range(0, HALF, LANES):
-        count = min(LANES, HALF - start)
-        line = index[pl.program_id(0), :, start : start + LANES]
-        wanted = jnp.broadcast_to(line, (LANES, LANES)).T[:count]
-        wanted = jnp.concatenate([wanted] * (columns // LANES), axis=1)
-        lines = slice(start, start + count)
-        out[lines, :] = jnp.where(wanted == here[:count], 0.0, out[lines, :])
+            for i in range(8 // STEPS):
+                block = step * (8 // STEPS) + i
+                product = lax.dot_general(
+                    wide(block // 4, block % 4), store[...], (((1,), (1,)), ((), ())),
+                    preferred_element_type=jnp.float32,
+                )
+                hit = wanted(block) - here
+                lines = slice(i * HALF, (i + 1) * HALF)
+                for n in range(0, columns, LANES):
+                    lanes = slice(n, n + LANES)
+                    out[lines, lanes] = jnp.where(hit == n, 0.0, product[:, lanes])
 
 
 def score(first, w, store, index):
     columns, depth = store.shape
-    count = index.shape[0] * HALF
+    count = index.shape[0]
+    vmem = pl.BlockSpec(memory_space=pltpu.VMEM)
     return pl.pallas_call(
         score_kernel,
         out_shape=jax.ShapeDtypeStruct((count, columns), jnp.float32),
-        grid=(index.shape[0],),
-        in_specs=[
-            pl.BlockSpec(memory_space=pltpu.SMEM),
-            pl.BlockSpec(memory_space=pltpu.VMEM),
-            pl.BlockSpec(memory_space=pltpu.VMEM),
-            pl.BlockSpec(memory_space=pltpu.VMEM),
-        ],
-        out_specs=pl.BlockSpec((HALF, columns), lambda i: (i, 0)),
+        grid=(STEPS,),
+        in_specs=[pl.BlockSpec(memory_space=pltpu.SMEM), vmem, vmem, vmem],
+        out_specs=pl.BlockSpec((count // STEPS, columns), lambda i: (i, 0)),
         compiler_params=pltpu.CompilerParams(vmem_limit_bytes=24 << 20),
     )(first, w, store, index)
 
@@ -415,8 +441,7 @@
     first = (place * store_rows.shape[0]).astype(jnp.int32).reshape(1)
     w = project(slab_grads, basis, eigenvalues.reshape(8, LANES))
     w = w.reshape(2, 4, 4, 7 * BLOCK, LANES)
-    index = jnp.pad(slab_index.reshape(8, 1, HALF), ((0, 0), (0, 0), (0, 2 * LANES - HALF)))
-    return score(first, w, store_rows, index)
+    return score(first, w, store_rows, slab_index)
 
 
 def solution(mesh):

time: 143 us -> 141 us (0.986)
    pallas_call x1, Pallas kernels: 6.1 us -> 4.27 us  [score(): pl.pallas_call(score_kernel, out_shape=jax.ShapeDtypeStruct((count, colum...]
where the time goes in v3:
time: 141 us
  Pallas kernels  141 us (100%)
    pallas_call x1, Pallas kernels, project(): pl.pallas_call(project_kernel, out_shape=pltpu.VMEM((2, 4, 4, 7, 8, TILE,...  136 us
    pallas_call x1, Pallas kernels, score(): pl.pallas_call(score_kernel, out_shape=jax.ShapeDtypeStruct((count, colum...  4.27 us

profile of v3, /device:TPU:1, one launch (start us, length us, event | category | flops | bytes accessed | tf_op | source)
XLA Modules:
  0.0 140.6 jit_solution(13660565792958851612)
XLA Ops:
  0.0 0.0 copy-start
  0.0 0.0 copy-start.1
  0.0 136.3 %shard_map.55 = bf16[2,4,4,7,8,8,128]{6,5,4,3,2,1,0:T(8,128)(2,1)S(1)} custom-call(bf16[224,8192]{1,0:T(8,128)(2,1)} %g.1, bf16[8192,128]{1,0:T(8,128)(2,1)} %b.1, f32[8,128]{1,0:T(8,128)} %bitcast.4), custom_call_target="tpu_custom_call" | custom-call | tf_op jit(solution)/shard_map/pallas_call | solution.py:345
  136.3 0.0 copy-done
  136.3 0.0 copy-done.1
  136.3 4.3 %shard_map.56 = f32[1792,512]{1,0:T(8,128)} custom-call(s32[1]{0:T(128)} %bitcast.first, bf16[2,4,4,448,128]{4,3,2,1,0:T(8,128)(2,1)S(1)} %bitcast.3, bf16[512,1024]{1,0:T(8,128)(2,1)S(1)} %copy-done, s32[1792]{0:T(1024)S(1)} %copy-done.1), custom_call_target="tpu_custom_call" | custom-call | tf_op jit(solution)/shard_map/pallas_call | solution.py:428
Async XLA Ops:
  0.0 136.3 %copy-start = (bf16[512,1024]{1,0:T(8,128)(2,1)S(1)}, bf16[512,1024]{1,0:T(8,128)(2,1)}, u32[]{:S(2)}) copy-start(bf16[512,1024]{1,0:T(8,128)(2,1)} %store.1) | copy-start | bytes 3145732
  0.0 136.3 %copy-start.1 = (s32[1792]{0:T(1024)S(1)}, s32[1792]{0:T(1024)}, u32[]{:S(2)}) copy-start(s32[1792]{0:T(1024)} %index.1) | copy-start | bytes 21508

commit v4 on v3

--- a/solution.py
+++ b/solution.py
@@ -14,6 +14,7 @@
 LANES = 128
 TILE = 8
 BLOCK = 64
+ROUNDS = 3
 TURNS = (0, -1, 1, 2)
 NEAR_ROWS = ((0, 32), (32, 96), (96, 160))
 LAST_ROWS = (160, 224)
@@ -28,7 +29,7 @@
 def project_kernel(
     g, b, eig_in, w,
     eig, g_own, g_pair, b_all, acc, r1, s1, r2, w0, w1, w2, w3,
-    local_sem, g_send, g_recv, b_send, b_recv, f_send, f_recv,
+    ready, local_sem, g_send, g_recv, b_send, b_recv, f_send, f_recv,
     a_send, a_recv, c_send, c_recv, e_send, e_recv, h_send, h_recv, k_send, k_recv,
 ):
     rows, feats = g.shape
@@ -56,13 +57,14 @@
         return {"x": turned("x", o[0]), "y": turned("y", o[1])}
 
     barrier = pltpu.get_barrier_semaphore()
-    everyone = (
-        [column_peer(o) for o in column]
-        + [sheet_peer(o) for o in sheet]
-        + [plane_peer(o) for o in plane if o[1]]
-    )
-    for peer in everyone:
-        pl.semaphore_signal(barrier, inc=1, device_id=peer, device_id_type=MESH)
+    beside = {"zl": 1 - zl, "zh": lax.rem(zh + 2 * zl + 3, 4)}
+    nearest = [pair, right, left, {"y": turned("y", 1)}, {"y": turned("y", -1)}, beside, sibling]
+
+    def meet(semaphore):
+        for peer in nearest:
+            pl.semaphore_signal(semaphore, inc=1, device_id=peer, device_id_type=MESH)
+
+    meet(barrier)
     locals_ = [
         pltpu.make_async_copy(b, b_all.at[0], local_sem.at[0]),
         pltpu.make_async_copy(g, g_own, local_sem.at[1]),
@@ -70,7 +72,7 @@
     ]
     for copy in locals_:
         copy.start()
-    pl.semaphore_wait(barrier, len(everyone))
+    pl.semaphore_wait(barrier, len(nearest))
 
     def remote(src, dst, send, recv, peer):
         return pltpu.make_async_remote_copy(
@@ -110,6 +112,10 @@
         b_copy(0, k).start()
         b_copy(1, k).start()
         last_copy(k).start()
+
+    for r in range(ROUNDS):
+        meet(ready.at[r])
+        pl.semaphore_wait(ready.at[r], len(nearest))
 
     def dot(lhs, rhs):
         out = jnp.dot(lhs, rhs, preferred_element_type=jnp.float32)
@@ -224,17 +230,40 @@
 
         guarded(within(zh, batch), body)
 
-    def spread_sheet(n):
-        batch = BATCHES[n]
+    def spread(n, place, peers, first):
+        return [
+            go(remote(
+                place, place, h_send.at[n, first + i], h_recv.at[n, first + i], peer
+            ))
+            for i, peer in enumerate(peers)
+        ]
+
+    def settle_column(n):
         for i, (_, dh) in enumerate(column):
             guarded(
-                within(turned("zh", -dh), batch), lambda i=i: column_arrival(n, i).wait_recv()
+                within(turned("zh", -dh), BATCHES[n]),
+                lambda i=i: column_arrival(n, i).wait_recv(),
             )
-        place = parts[n].at[x, mine]
-        return [
-            go(remote(place, place, h_send.at[n, i], h_recv.at[n, i], sheet_peer(o)))
-            for i, o in enumerate(sheet)
-        ]
+
+    def spread_sheet(n):
+        settle_column(n)
+        return spread(n, parts[n].at[x, mine], [sheet_peer(o) for o in sheet], 0)
+
+    x_peers = [{"x": turned("x", d)} for d in deep]
+    y_peers = [{"y": turned("y", d)} for d in deep]
+
+    def spread_first(n):
+        settle_column(n)
+        part = parts[n]
+        return spread(n, part.at[x, mine, 0], x_peers, 0) + spread(n, part.at[x, mine, 1], y_peers, 3)
+
+    def spread_second(n, copies):
+        for copy in copies:
+            copy.wait_recv()
+        part = parts[n]
+        return spread(n, part.at[:, mine, 0], y_peers, 6) + spread(
+            n, part.at[x, pl.ds(core * 4, 4), 1], x_peers, 9
+        )
 
     def share(n, copies):
         for copy in copies:
@@ -253,14 +282,16 @@
                 for p in range(low, high):
                     w[q, p, row, first:last, lot] = parts[n][row, lot, q, p - low]
 
+    @pl.loop(0, CHUNKS)
+    def _(k):
+        b_copy(0, k).wait_recv()
+        b_copy(1, k).wait_recv()
+        add_own(k, joined(range(3), k), slice(0, 3 * LANES))
+
     @pl.loop(0, CHUNKS // 2)
     def _(pairs):
         for odd in (0, 1):
-            k = pairs * 2 + odd
-            b_copy(0, k).wait_recv()
-            b_copy(1, k).wait_recv()
-            forward(odd, k).start()
-            add_own(k, joined(range(3), k), slice(0, 3 * LANES))
+            forward(odd, pairs * 2 + odd).start()
 
     near_copy(0).wait_recv()
     near_copy(1).wait_recv()
@@ -270,8 +301,6 @@
         add_pair(k, joined(range(3), k), slice(0, 3 * LANES))
 
     early = reduce_plane(0)
-    reduce_deep(0, early)
-    spread_column(0)
 
     @pl.loop(0, CHUNKS)
     def _(k):
@@ -287,7 +316,7 @@
         add_block(5, k)
 
     fifth = reduce_plane(2)
-    early = spread_sheet(0)
+    reduce_deep(0, early)
     reduce_deep(1, across)
     reduce_deep(2, fifth)
 
@@ -297,20 +326,26 @@
         add_block(6, k)
 
     sixth = reduce_plane(3)
+    spread_column(0)
     spread_column(1)
     spread_column(2)
     reduce_deep(3, sixth)
-    across = spread_sheet(1)
-    fifth = spread_sheet(2)
+    early = spread_first(0)
+    across = spread_first(1)
+    fifth = spread_first(2)
     spread_column(3)
+    early = spread_second(0, early)
+    across = spread_second(1, across)
+    fifth = spread_second(2, fifth)
+    sixth = spread_sheet(3)
     early = share(0, early)
-    sixth = spread_sheet(3)
     place_tiles(0, early)
     across = share(1, across)
     fifth = share(2, fifth)
+    sixth = share(3, sixth)
     place_tiles(1, across)
     place_tiles(2, fifth)
-    place_tiles(3, share(3, sixth))
+    place_tiles(3, sixth)
 
     for i in range(3):
         near_copy(i).wait_send()
@@ -360,6 +395,7 @@
                 pltpu.VMEM((4, 8, 2, high - low, last - first, TILE, LANES), bf16)
                 for first, last, low, high in BATCHES
             ),
+            pltpu.SemaphoreType.REGULAR((ROUNDS,)),
             dma((3,)),
             dma((3 + CHUNKS,)), dma((3 + CHUNKS,)),
             dma((2, CHUNKS)), dma((2, CHUNKS)),

time: 141 us -> 124 us (0.88)
  Pallas kernels: 141 us -> 124 us
    pallas_call x1, Pallas kernels: 136 us -> 119 us  [project(): pl.pallas_call(project_kernel, out_shape=pltpu.VMEM((2, 4, 4, 7, 8, TILE,...]
where the time goes in v4:
time: 124 us
  Pallas kernels  124 us (100%)
    pallas_call x1, Pallas kernels, project(): pl.pallas_call(project_kernel, out_shape=pltpu.VMEM((2, 4, 4, 7, 8, TILE,...  119 us
    pallas_call x1, Pallas kernels, score(): pl.pallas_call(score_kernel, out_shape=jax.ShapeDtypeStruct((count, colum...  4.27 us

profile of v4, /device:TPU:1, one launch (start us, length us, event | category | flops | bytes accessed | tf_op | source)
XLA Modules:
  0.0 123.6 jit_solution(14123204293746446277)
XLA Ops:
  0.0 0.0 copy-start
  0.0 0.0 copy-start.1
  0.0 119.3 %shard_map.55 = bf16[2,4,4,7,8,8,128]{6,5,4,3,2,1,0:T(8,128)(2,1)S(1)} custom-call(bf16[224,8192]{1,0:T(8,128)(2,1)} %g.1, bf16[8192,128]{1,0:T(8,128)(2,1)} %b.1, f32[8,128]{1,0:T(8,128)} %bitcast.4), custom_call_target="tpu_custom_call" | custom-call | tf_op jit(solution)/shard_map/pallas_call | solution.py:380
  119.3 0.0 copy-done
  119.3 0.0 copy-done.1
  119.3 4.3 %shard_map.56 = f32[1792,512]{1,0:T(8,128)} custom-call(s32[1]{0:T(128)} %bitcast.first, bf16[2,4,4,448,128]{4,3,2,1,0:T(8,128)(2,1)S(1)} %bitcast.3, bf16[512,1024]{1,0:T(8,128)(2,1)S(1)} %copy-done, s32[1792]{0:T(1024)S(1)} %copy-done.1), custom_call_target="tpu_custom_call" | custom-call | tf_op jit(solution)/shard_map/pallas_call | solution.py:464
Async XLA Ops:
  0.0 119.3 %copy-start = (bf16[512,1024]{1,0:T(8,128)(2,1)S(1)}, bf16[512,1024]{1,0:T(8,128)(2,1)}, u32[]{:S(2)}) copy-start(bf16[512,1024]{1,0:T(8,128)(2,1)} %store.1) | copy-start | bytes 3145732
  0.0 119.3 %copy-start.1 = (s32[1792]{0:T(1024)S(1)}, s32[1792]{0:T(1024)}, u32[]{:S(2)}) copy-start(s32[1792]{0:T(1024)} %index.1) | copy-start | bytes 21508

commit v5 on v4

--- a/solution.py
+++ b/solution.py
@@ -413,7 +413,7 @@
 
 
 HALF = 224
-STEPS = 4
+STEPS = 2
 
 
 def score_kernel(first, w, store, index, out):

time: 124 us -> 123 us (level)
  no operation moved by 1% of the time
where the time goes in v5:
time: 123 us
  Pallas kernels  123 us (100%)
    pallas_call x1, Pallas kernels, project(): pl.pallas_call(project_kernel, out_shape=pltpu.VMEM((2, 4, 4, 7, 8, TILE,...  119 us
    pallas_call x1, Pallas kernels, score(): pl.pallas_call(score_kernel, out_shape=jax.ShapeDtypeStruct((count, colum...  4.07 us

profile of v5, /device:TPU:1, one launch (start us, length us, event | category | flops | bytes accessed | tf_op | source)
XLA Modules:
  0.0 123.4 jit_solution(12923998128420017677)
XLA Ops:
  0.0 0.0 copy-start
  0.0 0.0 copy-start.1
  0.0 119.3 %shard_map.55 = bf16[2,4,4,7,8,8,128]{6,5,4,3,2,1,0:T(8,128)(2,1)S(1)} custom-call(bf16[224,8192]{1,0:T(8,128)(2,1)} %g.1, bf16[8192,128]{1,0:T(8,128)(2,1)} %b.1, f32[8,128]{1,0:T(8,128)} %bitcast.4), custom_call_target="tpu_custom_call" | custom-call | tf_op jit(solution)/shard_map/pallas_call | solution.py:380
  119.3 0.0 copy-done
  119.3 0.0 copy-done.1
  119.3 4.1 %shard_map.56 = f32[1792,512]{1,0:T(8,128)} custom-call(s32[1]{0:T(128)} %bitcast.first, bf16[2,4,4,448,128]{4,3,2,1,0:T(8,128)(2,1)S(1)} %bitcast.3, bf16[512,1024]{1,0:T(8,128)(2,1)S(1)} %copy-done, s32[1792]{0:T(1024)S(1)} %copy-done.1), custom_call_target="tpu_custom_call" | custom-call | tf_op jit(solution)/shard_map/pallas_call | solution.py:464
Async XLA Ops:
  0.0 119.3 %copy-start = (bf16[512,1024]{1,0:T(8,128)(2,1)S(1)}, bf16[512,1024]{1,0:T(8,128)(2,1)}, u32[]{:S(2)}) copy-start(bf16[512,1024]{1,0:T(8,128)(2,1)} %store.1) | copy-start | bytes 3145732
  0.0 119.3 %copy-start.1 = (s32[1792]{0:T(1024)S(1)}, s32[1792]{0:T(1024)}, u32[]{:S(2)}) copy-start(s32[1792]{0:T(1024)} %index.1) | copy-start | bytes 21508
